TPU v7x, 128 devices: a whole 4x4x4 slice. The times are simulated.
128 devices in a mesh: ctx: 16 (over y_hi, x, core), head: 8 (over y_lo, z).
Axes of the slice: x: 4, y: 4 (y_hi: 2, y_lo: 2; y = y_hi * 2 + y_lo), z: 4, core: 2. Of those that a mesh axis runs over, the one named last changes fastest.
Arguments:
- block_order: int32 [32], replicated, may hold values from 0 to 31, each once
- queries: bfloat16 [3584, 64, 576], P('ctx', 'head'), may hold values from -10 to 10
- keys: bfloat16 [3584, 576], P('ctx'), may hold values from -4 to 4
- dout: bfloat16 [3584, 64, 512], P('ctx', 'head'), may hold values from -6 to 6
Outputs:
- grad_queries: bfloat16 [3584, 64, 576], P('ctx', 'head')
- grad_keys: float32 [3584, 576], P('ctx')
Inputs may be any that keep to these rules, and one draw needn't show every extreme that they name: block_order holds each of 0 to 31 once.
All inputs are finite; a program needn't handle non-finite values.
Results may differ from a plain program's by a relative error of at most 0.0048.
Values may be sent and summed in bfloat16 or wider, within the bound.
A program may use at most 64 MiB of HBM per device.

v0:
```python
import jax
import jax.numpy as jnp
from jax import lax
from jax.sharding import PartitionSpec as P

softmax_scale = 0.1352
masked_value = -1e30


def per_device(block_order, queries, keys, dout):
    token_count, head_count, key_width = queries.shape
    latent_width = dout.shape[2]
    block_rows = token_count // 2
    ctx_index = lax.axis_index("ctx")
    offsets = jnp.arange(block_rows, dtype=jnp.int32)
    all_positions = (block_order[:, None] * block_rows + offsets[None, :]).reshape(-1)
    own_positions = lax.dynamic_slice_in_dim(all_positions, ctx_index * token_count, token_count)
    row_positions = jnp.repeat(own_positions, head_count)
    query_last = jnp.max(own_positions)
    query_rows = queries.reshape(token_count * head_count, key_width)
    grad_rows = dout.reshape(token_count * head_count, latent_width)
    row_count = query_rows.shape[0]
    seq_length = token_count * lax.axis_size("ctx")
    contract_rows = (((0,), (0,)), ((), ()))

    def block_scores(key_block, key_pos):
        scores = (
            jnp.dot(query_rows, key_block.T, preferred_element_type=jnp.float32) * softmax_scale
        )
        return jnp.where(key_pos[None, :] <= row_positions[:, None], scores, masked_value)

    def split_piece(piece):
        count = piece.shape[0] // token_count
        return (
            piece.reshape(count, token_count, key_width),
            all_positions.reshape(count, token_count),
        )

    def make_second(peak, total, delta):

        def second_fold(carry, piece, start):
            grad_query, grad_keys = carry
            blocks, positions = split_piece(piece)

            def second_visit(accum, items):
                key_block, key_pos = items

                def second_compute(accum):
                    scores = block_scores(key_block, key_pos)
                    probs = jnp.exp(scores - peak[:, None]) / total[:, None]
                    grad_probs = jnp.dot(
                        grad_rows, key_block[:, :latent_width].T, preferred_element_type=jnp.float32
                    )
                    grad_scores = (probs * (grad_probs - delta[:, None])).astype(jnp.bfloat16)
                    probs_half = probs.astype(jnp.bfloat16)
                    accum = (
                        accum
                        + jnp.dot(grad_scores, key_block, preferred_element_type=jnp.float32)
                        * softmax_scale
                    )
                    key_part = (
                        lax.dot_general(
                            grad_scores,
                            query_rows,
                            contract_rows,
                            preferred_element_type=jnp.float32,
                        )
                        * softmax_scale
                    )
                    value_part = lax.dot_general(
                        probs_half, grad_rows, contract_rows, preferred_element_type=jnp.float32
                    )
                    return (
                        accum,
                        key_part + jnp.pad(value_part, ((0, 0), (0, key_width - latent_width))),
                    )

                def skip(accum):
                    return (accum, jnp.zeros((token_count, key_width), jnp.float32))

                return lax.cond(jnp.min(key_pos) <= query_last, second_compute, skip, accum)

            grad_query, key_terms = lax.scan(second_visit, grad_query, (blocks, positions))
            length = piece.shape[0]
            grad_keys = key_terms.reshape(length, key_width)
            return (grad_query, grad_keys)

        return second_fold

    start_state = (
        jnp.full((row_count,), masked_value, jnp.float32),
        jnp.zeros((row_count,), jnp.float32),
        jnp.zeros((row_count,), jnp.float32),
    )
    second_start = (
        jnp.zeros((row_count, key_width), jnp.float32),
        jnp.zeros((seq_length, key_width), jnp.float32),
    )
    carry = start_state
    blocks, positions = split_piece(lax.all_gather(keys, "ctx", axis=0, tiled=True))

    def first_visit(state, items):
        key_block, key_pos = items

        def first_compute(state):
            peak, total, weighted = state
            scores = block_scores(key_block, key_pos)
            grad_probs = jnp.dot(
                grad_rows, key_block[:, :latent_width].T, preferred_element_type=jnp.float32
            )
            new_peak = jnp.maximum(peak, jnp.max(scores, axis=1))
            factor = jnp.exp(peak - new_peak)
            weights = jnp.exp(scores - new_peak[:, None])
            total = total * factor + jnp.sum(weights, axis=1)
            weighted = weighted * factor + jnp.sum(weights * grad_probs, axis=1)
            return (new_peak, total, weighted)

        def keep(state):
            return state

        return (lax.cond(jnp.min(key_pos) <= query_last, first_compute, keep, state), None)

    carry, unused = lax.scan(first_visit, carry, (blocks, positions))
    peak, total, weighted = carry
    second_fold = make_second(peak, total, weighted / total)
    grad_query, grad_keys = second_fold(
        second_start, lax.all_gather(keys, "ctx", axis=0, tiled=True), jnp.int32(0)
    )
    grad_queries = grad_query.reshape(token_count, head_count, key_width).astype(jnp.bfloat16)
    own_terms = lax.psum_scatter(grad_keys, "ctx", scatter_dimension=0, tiled=True)
    key_result = lax.psum(own_terms, "head")
    return (grad_queries, key_result)


def solution(mesh):
    placed = (P(), P("ctx", "head", None), P("ctx", None), P("ctx", "head", None))
    return jax.shard_map(
        per_device,
        mesh=mesh,
        in_specs=placed,
        out_specs=(P("ctx", "head", None), P("ctx", None)),
        check_vma=False,
    )
```

profile of v0, /device:TPU:0, one launch (start us, length us, event | category | flops | bytes accessed | tf_op | source)
XLA Modules:
  0.0 600.4 jit_solution(2105240949158212985)
XLA Ops:
  9.9 60.6 %all-gather.2.cloned.1.call-done = bf16[3584,576]{1,0:T(8,128)(2,1)} async-done(((bf16[224,576]{1,0:T(8,128)(2,1)}), bf16[3584,576]{1,0:T(8,128)(2,1)}) %all-gather.2.cloned.1.call-update) | async-done | bytes 4128784 | tf_op jit(solution)/shard_map/all_gather | solution.py:127
  70.5 69.5 %while.31 = (s32[]{:T(128)}, f32[1792]{0:T(1024)S(1)}, f32[1792]{0:T(1024)S(1)}, f32[1792]{0:T(1024)S(1)}, s32[16,224]{1,0:T(8,128)S(1)}, /*index=5*/s32[]{:T(12...) while((s32[]{:T(128)}, f32[1792]{0:T(1024)S(1)}, ...), condition=%wide.region_8.9_spmd.clone, body=%wide.region_1.8_spmd.clone.sunk | while | flops 877082112 | bytes 17222444 | solution.py:123
  72.4 5.0 conditional.6
  73.6 2.7 fusion.26
  79.2 5.0 conditional.6
  80.4 2.7 fusion.26
  86.0 5.0 conditional.6
  87.2 2.7 fusion.26
  98.4 5.0 conditional.6
  99.7 2.7 fusion.26
  105.3 5.0 conditional.6
  106.5 2.7 fusion.26
  112.1 5.0 conditional.6
  113.3 2.7 fusion.26
  126.4 5.0 conditional.6
  127.6 2.7 fusion.26
  135.1 5.0 conditional.6
  136.3 2.7 fusion.26
  142.3 136.9 %while.32 = (s32[]{:T(128)}, f32[1792,576]{0,1:T(8,128)}, f32[16,224,576]{2,1,0:T(8,128)}, s32[16,224]{1,0:T(8,128)S(1)}, s32[]{:T(128)}, /*index=5*/bf16[16,224...) while((s32[]{:T(128)}, f32[1792,576]{0,1:T(8,128)}, ...), condition=%wide.region_13.14_spmd.clone, body=%wide.region_9.13_spmd.clone.sunk | while | flops 2215284992 | bytes 68409680 | solution.py:83
  144.2 11.5 %conditional.7 = (f32[1792,576]{0,1:T(8,128)}, f32[1,224,576]{2,1,0:T(8,128)S(1)}) conditional(s32[]{:T(128)} %convert_element_type.32, f32[1792,576]{0,1:T(8,128)} %get-tuple-element.560, (s32[1,224]{1,0:T(1,128)S(1)}, s32[224]{0:T(256)S(1)}, bf16[16,224,576]{2,1,0:T(8,128)(2,1)}, s32[]{:T(128)}, bf16[1792,576]{1,0:T(8,128)(2,1)}, ...), branch_computations={%region_11.11_spmd, %region_12.12_spmd} | conditional | flops 2215284736 | bytes 67317608 | solution.py:81
  145.4 2.6 fusion.17
  158.4 11.5 %conditional.7 = (f32[1792,576]{0,1:T(8,128)}, f32[1,224,576]{2,1,0:T(8,128)S(1)}) conditional(s32[]{:T(128)} %convert_element_type.32, f32[1792,576]{0,1:T(8,128)} %get-tuple-element.560, (s32[1,224]{1,0:T(1,128)S(1)}, s32[224]{0:T(256)S(1)}, bf16[16,224,576]{2,1,0:T(8,128)(2,1)}, s32[]{:T(128)}, bf16[1792,576]{1,0:T(8,128)(2,1)}, ...), branch_computations={%region_11.11_spmd, %region_12.12_spmd} | conditional | flops 2215284736 | bytes 67317608 | solution.py:81
  172.7 11.5 %conditional.7 = (f32[1792,576]{0,1:T(8,128)}, f32[1,224,576]{2,1,0:T(8,128)S(1)}) conditional(s32[]{:T(128)} %convert_element_type.32, f32[1792,576]{0,1:T(8,128)} %get-tuple-element.560, (s32[1,224]{1,0:T(1,128)S(1)}, s32[224]{0:T(256)S(1)}, bf16[16,224,576]{2,1,0:T(8,128)(2,1)}, s32[]{:T(128)}, bf16[1792,576]{1,0:T(8,128)(2,1)}, ...), branch_computations={%region_11.11_spmd, %region_12.12_spmd} | conditional | flops 2215284736 | bytes 67317608 | solution.py:81
  173.9 2.6 fusion.17
  195.5 11.5 %conditional.7 = (f32[1792,576]{0,1:T(8,128)}, f32[1,224,576]{2,1,0:T(8,128)S(1)}) conditional(s32[]{:T(128)} %convert_element_type.32, f32[1792,576]{0,1:T(8,128)} %get-tuple-element.560, (s32[1,224]{1,0:T(1,128)S(1)}, s32[224]{0:T(256)S(1)}, bf16[16,224,576]{2,1,0:T(8,128)(2,1)}, s32[]{:T(128)}, bf16[1792,576]{1,0:T(8,128)(2,1)}, ...), branch_computations={%region_11.11_spmd, %region_12.12_spmd} | conditional | flops 2215284736 | bytes 67317608 | solution.py:81
  209.8 11.5 %conditional.7 = (f32[1792,576]{0,1:T(8,128)}, f32[1,224,576]{2,1,0:T(8,128)S(1)}) conditional(s32[]{:T(128)} %convert_element_type.32, f32[1792,576]{0,1:T(8,128)} %get-tuple-element.560, (s32[1,224]{1,0:T(1,128)S(1)}, s32[224]{0:T(256)S(1)}, bf16[16,224,576]{2,1,0:T(8,128)(2,1)}, s32[]{:T(128)}, bf16[1792,576]{1,0:T(8,128)(2,1)}, ...), branch_computations={%region_11.11_spmd, %region_12.12_spmd} | conditional | flops 2215284736 | bytes 67317608 | solution.py:81
  224.0 11.5 %conditional.7 = (f32[1792,576]{0,1:T(8,128)}, f32[1,224,576]{2,1,0:T(8,128)S(1)}) conditional(s32[]{:T(128)} %convert_element_type.32, f32[1792,576]{0,1:T(8,128)} %get-tuple-element.560, (s32[1,224]{1,0:T(1,128)S(1)}, s32[224]{0:T(256)S(1)}, bf16[16,224,576]{2,1,0:T(8,128)(2,1)}, s32[]{:T(128)}, bf16[1792,576]{1,0:T(8,128)(2,1)}, ...), branch_computations={%region_11.11_spmd, %region_12.12_spmd} | conditional | flops 2215284736 | bytes 67317608 | solution.py:81
  249.7 11.5 %conditional.7 = (f32[1792,576]{0,1:T(8,128)}, f32[1,224,576]{2,1,0:T(8,128)S(1)}) conditional(s32[]{:T(128)} %convert_element_type.32, f32[1792,576]{0,1:T(8,128)} %get-tuple-element.560, (s32[1,224]{1,0:T(1,128)S(1)}, s32[224]{0:T(256)S(1)}, bf16[16,224,576]{2,1,0:T(8,128)(2,1)}, s32[]{:T(128)}, bf16[1792,576]{1,0:T(8,128)(2,1)}, ...), branch_computations={%region_11.11_spmd, %region_12.12_spmd} | conditional | flops 2215284736 | bytes 67317608 | solution.py:81
  266.8 11.5 %conditional.7 = (f32[1792,576]{0,1:T(8,128)}, f32[1,224,576]{2,1,0:T(8,128)S(1)}) conditional(s32[]{:T(128)} %convert_element_type.32, f32[1792,576]{0,1:T(8,128)} %get-tuple-element.560, (s32[1,224]{1,0:T(1,128)S(1)}, s32[224]{0:T(256)S(1)}, bf16[16,224,576]{2,1,0:T(8,128)(2,1)}, s32[]{:T(128)}, bf16[1792,576]{1,0:T(8,128)(2,1)}, ...), branch_computations={%region_11.11_spmd, %region_12.12_spmd} | conditional | flops 2215284736 | bytes 67317608 | solution.py:81
  268.1 2.6 fusion.17
  279.3 235.8 %reduce-scatter.2.cloned.1.call-done = f32[224,576]{1,0:T(8,128)} async-done(((f32[3584,576]{1,0:T(8,128)}), f32[224,576]{1,0:T(8,128)}) %reduce-scatter.2.cloned.1.call-update) | async-done | bytes 516112 | tf_op jit(solution)/shard_map/reduce_scatter | solution.py:130
  520.1 71.9 %all-reduce.3.cloned.1.call-done = f32[224,576]{1,0:T(8,128)} async-done(((f32[224,576]{1,0:T(8,128)}), f32[224,576]{1,0:T(8,128)}) %all-reduce.3.cloned.1.call-update) | async-done | bytes 516112 | tf_op jit(solution)/shard_map/psum | solution.py:131
  (288 shorter events, 148.4 us)
Async XLA Ops:
  7.2 63.4 %all-gather.2.cloned.1.call-start = ((), (), s32[]{:S(2)}) async-start(), calls=%async_computation.1 | async-start | bytes 4874240 | tf_op jit(solution)/shard_map/all_gather | solution.py:127
  7.9 507.2 %reduce-scatter.2.cloned.1.call-start = ((), (), s32[]{:S(2)}) async-start(), calls=%async_computation.2 | async-start | bytes 9748480 | tf_op jit(solution)/shard_map/reduce_scatter | solution.py:130
  73.6 2.7 copy-start.2
  80.4 2.7 copy-start.2
  87.2 2.7 copy-start.2
  99.6 2.7 copy-start.2
  106.5 2.7 copy-start.2
  113.3 2.7 copy-start.2
  127.6 2.7 copy-start.2
  136.3 2.7 copy-start.2
  140.1 2.2 copy-start.3
  148.6 1.6 copy-start.4
  150.3 2.2 copy-start
  153.8 1.9 copy-start.1
  162.9 1.6 copy-start.4
  164.5 2.2 copy-start
  168.0 1.9 copy-start.1
  177.1 1.6 copy-start.4
  178.8 2.2 copy-start
  182.2 1.9 copy-start.1
  200.0 1.6 copy-start.4
  201.6 2.2 copy-start
  205.1 1.9 copy-start.1
  215.9 2.2 copy-start
  219.3 1.9 copy-start.1
  230.1 2.2 copy-start
  233.6 1.9 copy-start.1
  255.8 2.2 copy-start
  259.3 1.9 copy-start.1
  272.9 2.2 copy-start
  276.4 1.9 copy-start.1
  279.2 312.7 %all-reduce.3.cloned.1.call-start = ((), (), s32[]{:S(2)}) async-start(), calls=%async_computation.3 | async-start | bytes 1146880 | tf_op jit(solution)/shard_map/psum | solution.py:131
  (4 other events, 6.6 us)
Sparse Core Ops, SparseCore 0:
  10.4 60.0 all-gather.1
  279.4 235.7 reduce-scatter.1
  517.6 74.2 all-reduce.2
where the time goes:
time: 604 us; the launch traced here: 600 us
  waiting for transfers between devices  369 us (61%)
  matrix products  76.1 us (13%)
  local copies, waits for them, and re-layouts  73.3 us (12%)
  loops' own time  41.3 us (7%)
  other arithmetic  26.7 us (4%)
  between operations  13.8 us (2%)
    reduce_scatter x1, waiting for transfers between devices, per_device(): lax.psum_scatter(grad_keys, 'ctx', scatter_dimension=0, tiled=True)  236 us
    psum x1, waiting for transfers between devices, per_device(): key_result = lax.psum(own_terms, 'head')  71.9 us
    all_gather x1, waiting for transfers between devices, per_device(): lax.all_gather(keys, 'ctx', axis=0, tiled=True)  60.6 us
    dot_general x16, matrix products, block_scores(): jnp.dot(query_rows, key_block.T, preferred_element_type=jnp.float32)  42 us
    cond x72, local copies, waits for them, and re-layouts  33.2 us
    another operation x1, loops' own time, second_fold(): lax.scan(second_visit, grad_query, (blocks, positions))  20.3 us
    another operation x1, loops' own time, per_device(): carry, unused = lax.scan(first_visit, carry, (blocks, positions))  19.4 us
    squeeze x16, local copies, waits for them, and re-layouts, per_device(): carry, unused = lax.scan(first_visit, carry, (blocks, positions))  15.8 us
  transfers between devices with their start and end apart: 3, of which 3 were waited for; matrix products, arithmetic and copies ran while one was open for 1% of the time, Pallas kernels for 0%

commit v1 on v0

v1 whole, which is shorter than its diff:
```python
import functools

import jax
import jax.numpy as jnp
from jax import lax
from jax.experimental import pallas as pl
from jax.experimental.pallas import tpu as pltpu
from jax.sharding import PartitionSpec as P

SCALE = 0.1352
LOG2E = 1.4426950408889634
EXP_SCALE = SCALE * LOG2E
NEG = -1e30
LAT = 512
MESH = pl.DeviceIdType.MESH
BF16, F32 = jnp.bfloat16, jnp.float32


def dot_nt(a, b):
    return lax.dot_general(a, b, (((1,), (1,)), ((), ())), preferred_element_type=F32)


def dot_tn(a, b):
    return lax.dot_general(a, b, (((0,), (0,)), ((), ())), preferred_element_type=F32)


def dot(a, b):
    return jnp.dot(a, b, preferred_element_type=F32)


def aligned(index, size):
    return pl.ds(pl.multiple_of(index * size, size), size)


def where_am_i():
    ctx, head = lax.axis_index("ctx"), lax.axis_index("head")
    return ctx // 8, lax.rem(ctx // 2, 4), lax.rem(ctx, 2), head // 4, lax.rem(head, 4)


def place(y_hi, x, core, y_lo, z):
    return {"ctx": y_hi * 8 + x * 2 + core, "head": y_lo * 4 + z}


def greet(peers):
    barrier = pltpu.get_barrier_semaphore()
    for peer in peers:
        pl.semaphore_signal(barrier, inc=1, device_id=peer, device_id_type=MESH)
    pl.semaphore_wait(barrier, len(peers))


def attention_kernel(
    sizes, order, own_ref, q_hbm, do_hbm, dq_hbm, dk_hbm,
    keys, q_ref, do_ref, sbuf, dpbuf, pt, dst, dk_buf, dq_buf,
    in_sem, send_sem, recv_sem, pass_sem, mate_sem, dk_sem, dq_sem,
):
    shard, rows, tile, chunk = sizes
    half = shard // 2
    n_keys = keys.shape[0]
    n_tiles, n_chunks, n_groups = rows // tile, n_keys // chunk, n_keys // half
    heads = rows // shard
    y_hi, x, core, y_lo, z = where_am_i()
    ctx = lax.axis_index("ctx")

    q_in = pltpu.make_async_copy(q_hbm, q_ref, in_sem.at[0])
    do_in = pltpu.make_async_copy(do_hbm, do_ref, in_sem.at[1])
    own_in = pltpu.make_async_copy(own_ref, keys.at[aligned(ctx, shard)], in_sem.at[2])
    own_in.start()
    q_in.start()
    do_in.start()

    mate = place(y_hi, x, 1 - core, y_lo, z)
    steps = [(0, 1), (0, 3), (1, 0), (0, 2), (1, 1), (1, 3), (1, 2)]

    def peer_of(dy, dx):
        there = (y_hi + dy) % 2, lax.rem(x + dx, 4)
        return place(*there, core, (y_lo + dy) % 2, z)

    def slot_from(dy, dx):
        return ((y_hi + dy) % 2) * 8 + lax.rem(x + 4 - dx, 4) * 2 + core

    greet([mate] + [peer_of(*step) for step in steps])
    own_in.wait()
    own_slot = keys.at[aligned(ctx, shard)]
    sends = []
    for n, step in enumerate(steps):
        sends.append(pltpu.make_async_remote_copy(
            src_ref=own_slot, dst_ref=own_slot, send_sem=send_sem.at[n], recv_sem=recv_sem.at[n],
            device_id=peer_of(*step), device_id_type=MESH))
    passes = []
    for n in range(len(steps) + 1):
        slot = keys.at[aligned(ctx if n == 0 else slot_from(*steps[n - 1]), shard)]
        passes.append(pltpu.make_async_remote_copy(
            src_ref=slot, dst_ref=slot, send_sem=pass_sem.at[n], recv_sem=mate_sem.at[n],
            device_id=mate, device_id_type=MESH))
    for send in sends:
        send.start()
    passes[0].start()
    for n in range(len(steps)):
        sends[n].wait_recv()
        passes[n + 1].start()
    q_in.wait()
    do_in.wait()
    for copy in passes:
        copy.wait_recv()

    pos_a, pos_b = order[2 * ctx], order[2 * ctx + 1]
    half_rows = rows // 2

    def lane_rows(t):
        return t * tile + lax.broadcasted_iota(jnp.int32, (1, tile), 1)

    def row_pos(t):
        return jnp.where(lane_rows(t) < half_rows, pos_a, pos_b)

    def fold(value, how):
        return how(value.reshape(value.shape[0] // 8, 8, tile), axis=0)

    def scores(t, slot):
        pos = row_pos(t)
        best = jnp.full((8, tile), NEG, F32)
        s = dot_nt(keys[...], q_ref[aligned(t, tile), :])
        sbuf[slot] = s
        for g in range(n_groups):
            top = fold(s[g * half:(g + 1) * half], jnp.max)
            best = jnp.maximum(best, jnp.where(order[g] < pos, top, NEG))
        return best

    def diagonal(t, slot, best):
        own = aligned(ctx, shard)
        lanes = lane_rows(t)
        late = lanes >= half_rows
        offset = jnp.where(late, lanes - half_rows, lanes) // heads
        key = lax.broadcasted_iota(jnp.int32, (shard, 1), 0)
        key_late = key >= half
        key_off = jnp.where(key_late, key - half, key)
        same = key_late == late
        s = sbuf[slot, own, :]
        s = jnp.where(same & (key_off > offset), NEG, s)
        sbuf[slot, own, :] = s
        return jnp.maximum(best, fold(jnp.where(same, s, NEG), jnp.max))

    def weigh(t, slot, best):
        pos = row_pos(t)
        top = jnp.max(best, axis=0, keepdims=True) * EXP_SCALE
        total = jnp.zeros((8, tile), F32)
        mixed = jnp.zeros((8, tile), F32)
        for g in range(n_groups):
            span = pl.ds(g * half, half)
            shift = jnp.where(order[g] <= pos, top, -NEG)
            e = jnp.exp2(sbuf[slot, span, :] * EXP_SCALE - shift)
            sbuf[slot, span, :] = e
            total += fold(e, jnp.sum)
            mixed += fold(e * dpbuf[span, :], jnp.sum)
        scale = 1.0 / jnp.sum(total, axis=0, keepdims=True)
        return scale, jnp.sum(mixed, axis=0, keepdims=True) * scale

    def settle(t, slot, scale, delta):
        out = aligned(t, tile)
        p = sbuf[slot] * scale
        ds = p * (dpbuf[...] - delta)
        pt[:, out] = p.astype(BF16)
        dst[:, out] = ds.astype(BF16)

    def grad_probs(t):
        dpbuf[...] = dot_nt(keys[:, :LAT], do_ref[aligned(t, tile), :])

    best = diagonal(0, 0, scores(0, 0))
    grad_probs(0)

    def one_tile(t, best):
        slot = lax.rem(t, 2)
        later = scores(t + 1, 1 - slot)
        scale, delta = weigh(t, slot, best)
        later = diagonal(t + 1, 1 - slot, later)
        settle(t, slot, scale, delta)
        grad_probs(t + 1)
        return later

    best = lax.fori_loop(0, n_tiles - 1, one_tile, best)
    last = n_tiles - 1
    scale, delta = weigh(last, last % 2, best)
    settle(last, last % 2, scale, delta)

    def dk_out(i):
        return pltpu.make_async_copy(dk_buf.at[lax.rem(i, 2)], dk_hbm.at[aligned(i, chunk)], dk_sem.at[i])

    def dq_out(t):
        return pltpu.make_async_copy(dq_buf.at[lax.rem(t, 2)], dq_hbm.at[aligned(t, tile)], dq_sem.at[t])

    def key_chunk(i, carry):
        @pl.when(i >= 2)
        def _():
            dk_out(i - 2).wait()

        span = aligned(i, chunk)
        a = dot(dst[span, :], q_ref[...]) * SCALE
        b = dot(pt[span, :], do_ref[...])
        dk_buf[lax.rem(i, 2), :, :LAT] = (a[:, :LAT] + b).astype(BF16)
        dk_buf[lax.rem(i, 2), :, LAT:] = a[:, LAT:].astype(BF16)
        dk_out(i).start()
        return carry

    lax.fori_loop(0, n_chunks, key_chunk, 0)

    def query_tile(t, carry):
        @pl.when(t >= 2)
        def _():
            dq_out(t - 2).wait()

        dq_buf[lax.rem(t, 2)] = (dot_tn(dst[:, aligned(t, tile)], keys[...]) * SCALE).astype(BF16)
        dq_out(t).start()
        return carry

    lax.fori_loop(0, n_tiles, query_tile, 0)

    for send in sends:
        send.wait_send()
    for copy in passes:
        copy.wait_send()
    for i in (n_chunks - 2, n_chunks - 1):
        dk_out(i).wait()
    for t in (n_tiles - 2, n_tiles - 1):
        dq_out(t).wait()


def reduce_kernel(
    part, out_ref, mated, sums, x_far, z_far, a0, a1, z_near, x_near, part_y, from_y, part_t, from_t, final, from_z,
    mate_s, mate_r, x1_s, x1_r, z1_s, z1_r, x2_s, x2_r, z2_s, z2_r, y_s, y_r, t_s, t_r, g_s, g_r,
):
    shard, win = sums.shape[1], a0.shape[1]
    y_hi, x, core, y_lo, z = where_am_i()
    mate = place(y_hi, x, 1 - core, y_lo, z)
    xs = [lax.rem(x + d, 4) for d in range(4)]
    zs = [lax.rem(z + d, 4) for d in range(4)]
    x_peer = [place(y_hi, xs[d], core, y_lo, z) for d in range(4)]
    z_peer = [place(y_hi, x, core, y_lo, zs[d]) for d in range(4)]
    partner = place(1 - y_hi, x, core, 1 - y_lo, z)
    twin = place(y_hi, x, core, 1 - y_lo, z)
    greet([mate, partner, twin] + x_peer[1:] + z_peer[1:])

    def start_of(q):
        first = jnp.where(q == 0, 0, jnp.where(q == 1, 64, jnp.where(q == 2, 112, 160)))
        return pl.ds(pl.multiple_of(first, 16), win)

    def remote(src, dst, send, recv, device):
        return pltpu.make_async_remote_copy(
            src_ref=src, dst_ref=dst, send_sem=send, recv_sem=recv, device_id=device, device_id_type=MESH)

    pending = []

    def go(copy):
        copy.start()
        pending.append(copy)
        return copy

    order = [(g // 2) + 4 * (1 - g % 2) for g in range(8)]
    first = {g: go(remote(part.at[aligned(g * 2 + 1 - core, shard)], mated.at[g], mate_s.at[g], mate_r.at[g], mate)) for g in order}
    x1, z1 = [], []
    for g in order:
        first[g].wait_recv()
        own = part[aligned(g * 2 + core, shard), :].astype(F32)
        sums[g] = (own + mated[g].astype(F32)).astype(BF16)
        if g < 4:
            for d in (1, 3, 2):
                z1.append(go(remote(sums.at[g, start_of(zs[d])], z_far.at[d - 1, g], z1_s.at[d - 1, g], z1_r.at[d - 1, g], z_peer[d])))
    for d in (1, 3, 2):
        x1.append(go(remote(sums.at[4 + xs[d]], x_far.at[d - 1], x1_s.at[d - 1], x1_r.at[d - 1], x_peer[d])))

    for copy in z1:
        copy.wait_recv()
    for g in range(4):
        total = sums[g, start_of(z), :].astype(F32)
        for d in range(3):
            total += z_far[d, g].astype(F32)
        a0[g] = total.astype(BF16)
    x2 = [go(remote(a0.at[xs[d]], x_near.at[d - 1], x2_s.at[d - 1], x2_r.at[d - 1], x_peer[d])) for d in (1, 3, 2)]
    for copy in x1:
        copy.wait_recv()
    total = sums[4 + x].astype(F32)
    for d in range(3):
        total += x_far[d].astype(F32)
    a1[...] = total.astype(BF16)
    z2 = [go(remote(a1.at[start_of(zs[d])], z_near.at[d - 1], z2_s.at[d - 1], z2_r.at[d - 1], z_peer[d])) for d in (1, 3, 2)]

    for copy in x2 + z2:
        copy.wait_recv()
    low = a0[x].astype(F32)
    high = a1[start_of(z), :].astype(F32)
    for d in range(3):
        low += x_near[d].astype(F32)
        high += z_near[d].astype(F32)
    up = y_hi == 1
    part_y[...] = jnp.where(up, low, high)
    keep = jnp.where(up, high, low)
    go(remote(part_y, from_y, y_s, y_r, partner)).wait_recv()
    mine = keep + from_y[...]
    part_t[...] = mine
    go(remote(part_t, from_t, t_s, t_r, twin)).wait_recv()
    final[...] = mine + from_t[...]
    last = [go(remote(final, from_z.at[d - 1], g_s.at[d - 1], g_r.at[d - 1], z_peer[d])) for d in (1, 3, 2)]

    for copy in last:
        copy.wait_recv()
    for q, (lo, hi) in enumerate(((0, 64), (64, 112), (112, 160), (160, 224))):
        d = lax.rem(z - q + 4, 4)
        value = final[0:hi - lo]
        for k in range(1, 4):
            value = jnp.where(d == k, from_z[k - 1, 0:hi - lo, :], value)
        out_ref[lo:hi, :] = value
    for copy in pending:
        copy.wait_send()


def per_device(block_order, queries, keys, dout):
    shard, heads, width = queries.shape
    rows = shard * heads
    seq = shard * lax.axis_size("ctx")
    tile, chunk = 256, 2 * shard
    any_spec = pl.BlockSpec(memory_space=pl.ANY)
    vmem = pl.BlockSpec(memory_space=pltpu.VMEM)
    dma = pltpu.SemaphoreType.DMA
    grad_queries, partial = pl.pallas_call(
        functools.partial(attention_kernel, (shard, rows, tile, chunk)),
        out_shape=(jax.ShapeDtypeStruct((rows, width), BF16), jax.ShapeDtypeStruct((seq, width), BF16)),
        in_specs=[pl.BlockSpec(memory_space=pltpu.SMEM), any_spec, any_spec, any_spec],
        out_specs=[any_spec, any_spec],
        scratch_shapes=[
            pltpu.VMEM((seq, width), BF16),
            pltpu.VMEM((rows, width), BF16),
            pltpu.VMEM((rows, LAT), BF16),
            pltpu.VMEM((2, seq, tile), F32),
            pltpu.VMEM((seq, tile), F32),
            pltpu.VMEM((seq, rows), BF16),
            pltpu.VMEM((seq, rows), BF16),
            pltpu.VMEM((2, chunk, width), BF16),
            pltpu.VMEM((2, tile, width), BF16),
            dma((3,)), dma((7,)), dma((7,)), dma((8,)), dma((8,)), dma((seq // chunk,)), dma((rows // tile,)),
        ],
        compiler_params=pltpu.CompilerParams(collective_id=0, has_side_effects=True, vmem_limit_bytes=63 << 20),
    )(block_order, keys, queries.reshape(rows, width), dout.reshape(rows, LAT))
    win = 64
    key_result = pl.pallas_call(
        reduce_kernel,
        out_shape=jax.ShapeDtypeStruct((shard, width), F32),
        in_specs=[vmem],
        out_specs=vmem,
        scratch_shapes=[
            pltpu.VMEM((8, shard, width), BF16), pltpu.VMEM((8, shard, width), BF16),
            pltpu.VMEM((3, shard, width), BF16), pltpu.VMEM((3, 4, win, width), BF16),
            pltpu.VMEM((4, win, width), BF16), pltpu.VMEM((shard, width), BF16),
            pltpu.VMEM((3, win, width), BF16), pltpu.VMEM((3, win, width), BF16),
            pltpu.VMEM((win, width), F32), pltpu.VMEM((win, width), F32),
            pltpu.VMEM((win, width), F32), pltpu.VMEM((win, width), F32),
            pltpu.VMEM((win, width), F32), pltpu.VMEM((3, win, width), F32),
            dma((8,)), dma((8,)), dma((3,)), dma((3,)), dma((3, 4)), dma((3, 4)), dma((3,)), dma((3,)),
            dma((3,)), dma((3,)), dma, dma, dma, dma, dma((3,)), dma((3,)),
        ],
        compiler_params=pltpu.CompilerParams(collective_id=1, has_side_effects=True, vmem_limit_bytes=40 << 20),
    )(partial)
    return grad_queries.reshape(shard, heads, width), key_result


def solution(mesh):
    placed = (P(), P("ctx", "head", None), P("ctx", None), P("ctx", "head", None))
    return jax.shard_map(
        per_device,
        mesh=mesh,
        in_specs=placed,
        out_specs=(P("ctx", "head", None), P("ctx", None)),
        check_vma=False,
    )
```

time: 604 us -> 154 us (0.25)
  waiting for transfers between devices: 369 us -> 0 us
  Pallas kernels: 0 us -> 148 us
  matrix products: 76.1 us -> 0 us
  local copies, waits for them, and re-layouts: 73.3 us -> 4.49 us
  loops' own time: 41.3 us -> 0 us
  other arithmetic: 26.7 us -> 0 us
  between operations: 13.8 us -> 0.66 us
    reduce_scatter x1 -> x0, waiting for transfers between devices: 236 us -> none  [per_device(): lax.psum_scatter(grad_keys, 'ctx', scatter_dimension=0, tiled=True)]
    pallas_call x0 -> x2, Pallas kernels: none -> 148 us  [the longest x1 103 us: per_device(): pl.pallas_call(functools.partial(attention_kernel, (shard, rows, tile, ch...]
    dot_general x56 -> x0, matrix products: 76.1 us -> none  [the longest x16 42 us: block_scores(): jnp.dot(query_rows, key_block.T, preferred_element_type=jnp.float32)]
    psum x1 -> x0, waiting for transfers between devices: 71.9 us -> none  [per_device(): key_result = lax.psum(own_terms, 'head')]
    all_gather x1 -> x0, waiting for transfers between devices: 60.6 us -> none  [per_device(): lax.all_gather(keys, 'ctx', axis=0, tiled=True)]
    another operation x34 -> x0, loops' own time: 41.3 us -> none  [the longest x1 20.3 us: second_fold(): lax.scan(second_visit, grad_query, (blocks, positions))]
    cond x72 -> x0, local copies, waits for them, and re-layouts: 33.2 us -> none
    reduce_min x32 -> x0, other arithmetic: 20.8 us -> none  [the longest x16 10.5 us: second_visit(): return lax.cond(jnp.min(key_pos) <= query_last, second_compute, skip, accum)]
  transfers between devices with their start and end apart: 3 -> 0, of which waited for: 3 -> 0; matrix products, arithmetic and copies ran while one was open for 1% -> 0% of each run, Pallas kernels for 0% -> 0%
where the time goes in v1:
time: 154 us; the launch traced here: 153 us
  Pallas kernels  148 us (96%)
  local copies, waits for them, and re-layouts  4.49 us (3%)
    pallas_call x1, Pallas kernels, per_device(): pl.pallas_call(functools.partial(attention_kernel, (shard, rows, tile, ch...  103 us
    pallas_call x1, Pallas kernels, per_device(): pl.pallas_call(reduce_kernel, out_shape=jax.ShapeDtypeStruct((shard, widt...  44.8 us
    unnamed x6, local copies, waits for them, and re-layouts  4.49 us

profile of v1, /device:TPU:0, one launch (start us, length us, event | category | flops | bytes accessed | tf_op | source)
XLA Modules:
  0.0 153.1 jit_solution(3797865345702033338)
XLA Ops:
  0.6 103.1 %shard_map.59 = (bf16[1792,576]{1,0:T(8,128)(2,1)}, bf16[3584,576]{1,0:T(8,128)(2,1)}) custom-call(s32[32]{0:T(128)} %order.1, bf16[224,576]{1,0:T(8,128)(2,1)} %own_ref.1, bf16[1792,576]{1,0:T(8,128)(2,1)} %bitcast.3, bf16[1792,512]{1,0:T(8,128)(2,1)} %bitcast.5), custom_call_target="tpu_custom_call" | custom-call | tf_op jit(solution)/shard_map/pallas_call | solution.py:322
  103.7 0.0 copy-start
  103.7 2.3 %copy-done = bf16[3584,576]{1,0:T(8,128)(2,1)S(1)} copy-done((bf16[3584,576]{1,0:T(8,128)(2,1)S(1)}, bf16[3584,576]{1,0:T(8,128)(2,1)}, u32[]{:S(2)}) %copy-start) | copy-done | bytes 4128792
  106.0 0.0 copy-start.1
  106.0 44.8 %shard_map.60 = f32[224,576]{1,0:T(8,128)S(1)} custom-call(bf16[3584,576]{1,0:T(8,128)(2,1)S(1)} %copy-done), custom_call_target="tpu_custom_call" | custom-call | tf_op jit(solution)/shard_map/pallas_call | solution.py:342
  150.8 0.0 copy-done.1
  150.9 1.4 copy.8
  152.2 0.8 copy.9
Async XLA Ops:
  103.7 2.3 %copy-start = (bf16[3584,576]{1,0:T(8,128)(2,1)S(1)}, bf16[3584,576]{1,0:T(8,128)(2,1)}, u32[]{:S(2)}) copy-start(bf16[3584,576]{1,0:T(8,128)(2,1)} %get-tuple-element.5.part) | copy-start | bytes 12386308
  106.0 44.9 %copy-start.1 = (bf16[1792,576]{1,0:T(8,128)(2,1)S(1)}, bf16[1792,576]{1,0:T(8,128)(2,1)}, u32[]{:S(2)}) copy-start(bf16[1792,576]{1,0:T(8,128)(2,1)} %get-tuple-element.4) | copy-start | bytes 6193156

commit v2 on v1

v2 whole, which is shorter than its diff:
```python
import functools

import jax
import jax.numpy as jnp
from jax import lax
from jax.experimental import pallas as pl
from jax.experimental.pallas import tpu as pltpu
from jax.sharding import PartitionSpec as P

SCALE = 0.1352
LOG2E = 1.4426950408889634
EXP_SCALE = SCALE * LOG2E
NEG = -1e30
LAT = 512
STEP = 896
MESH = pl.DeviceIdType.MESH
BF16, F32 = jnp.bfloat16, jnp.float32


def dot_nt(a, b):
    return lax.dot_general(a, b, (((1,), (1,)), ((), ())), preferred_element_type=F32)


def dot_tn(a, b):
    return lax.dot_general(a, b, (((0,), (0,)), ((), ())), preferred_element_type=F32)


def dot(a, b):
    return jnp.dot(a, b, preferred_element_type=F32)


def aligned(index, size):
    return pl.ds(pl.multiple_of(index * size, size), size)


def where_am_i():
    ctx, head = lax.axis_index("ctx"), lax.axis_index("head")
    return ctx // 8, lax.rem(ctx // 2, 4), lax.rem(ctx, 2), head // 4, lax.rem(head, 4)


def place(y_hi, x, core, y_lo, z):
    return {"ctx": y_hi * 8 + x * 2 + core, "head": y_lo * 4 + z}


def greet(peers):
    barrier = pltpu.get_barrier_semaphore()
    for peer in peers:
        pl.semaphore_signal(barrier, inc=1, device_id=peer, device_id_type=MESH)
    pl.semaphore_wait(barrier, len(peers))


def attention_kernel(
    sizes, order, own_ref, q_hbm, do_hbm, dq_hbm, dk_ref,
    keys, q_ref, do_ref, sbuf, dpbuf, pt, dst, dq_buf,
    own_part, give, mated, sums, x_fwd, x_full, z_fwd, z_near, z_full, a0, a1, z_two, x_two, halves, from_y, final, from_z,
    in_sem, send_sem, recv_sem, pass_sem, mate_sem, dq_sem,
    m_s, m_r, xf_s, xf_r, xn_s, xn_r, zf_s, zf_r, zn_s, zn_r, x2_s, x2_r, z2_s, z2_r, y_s, y_r, g_s, g_r,
):
    shard, rows, tile, chunk, win = sizes
    half = shard // 2
    n_keys = keys.shape[0]
    n_tiles, n_groups = rows // tile, n_keys // half
    heads = rows // shard
    y_hi, x, core, y_lo, z = where_am_i()
    ctx = lax.axis_index("ctx")

    q_in = pltpu.make_async_copy(q_hbm, q_ref, in_sem.at[0])
    do_in = pltpu.make_async_copy(do_hbm, do_ref, in_sem.at[1])
    own_in = pltpu.make_async_copy(own_ref, keys.at[aligned(ctx, shard)], in_sem.at[2])
    own_in.start()
    q_in.start()
    do_in.start()

    mate = place(y_hi, x, 1 - core, y_lo, z)
    steps = [(0, 1), (0, 3), (1, 0), (0, 2), (1, 1), (1, 3), (1, 2)]

    def peer_of(dy, dx):
        there = (y_hi + dy) % 2, lax.rem(x + dx, 4)
        return place(*there, core, (y_lo + dy) % 2, z)

    def slot_from(dy, dx):
        return ((y_hi + dy) % 2) * 8 + lax.rem(x + 4 - dx, 4) * 2 + core

    x_peer = [place(y_hi, lax.rem(x + d, 4), core, y_lo, z) for d in range(4)]
    z_peer = [place(y_hi, x, core, y_lo, lax.rem(z + d, 4)) for d in range(4)]
    twin = place(y_hi, x, core, 1 - y_lo, z)
    across = [twin, place(1 - y_hi, x, core, 1 - y_lo, z), place(1 - y_hi, x, core, y_lo, z)]
    greet([mate, across[0], across[2]] + z_peer[1:] + [peer_of(*step) for step in steps])
    own_in.wait()
    own_slot = keys.at[aligned(ctx, shard)]
    sends = []
    for n, step in enumerate(steps):
        sends.append(pltpu.make_async_remote_copy(
            src_ref=own_slot, dst_ref=own_slot, send_sem=send_sem.at[n], recv_sem=recv_sem.at[n],
            device_id=peer_of(*step), device_id_type=MESH))
    passes = []
    for n in range(len(steps) + 1):
        slot = keys.at[aligned(ctx if n == 0 else slot_from(*steps[n - 1]), shard)]
        passes.append(pltpu.make_async_remote_copy(
            src_ref=slot, dst_ref=slot, send_sem=pass_sem.at[n], recv_sem=mate_sem.at[n],
            device_id=mate, device_id_type=MESH))
    for send in sends:
        send.start()
    passes[0].start()
    for n in range(len(steps)):
        sends[n].wait_recv()
        passes[n + 1].start()
    q_in.wait()
    do_in.wait()
    for copy in passes:
        copy.wait_recv()

    pos_a, pos_b = order[2 * ctx], order[2 * ctx + 1]
    half_rows = rows // 2

    def lane_rows(t):
        return t * tile + lax.broadcasted_iota(jnp.int32, (1, tile), 1)

    def row_pos(t):
        return jnp.where(lane_rows(t) < half_rows, pos_a, pos_b)

    def fold(value, how):
        return how(value.reshape(value.shape[0] // 8, 8, tile), axis=0)

    def scores(t, slot):
        pos = row_pos(t)
        best = jnp.full((8, tile), NEG, F32)
        for m in range(0, n_keys, STEP):
            s = dot_nt(keys[m:m + STEP, :], q_ref[aligned(t, tile), :])
            sbuf[slot, m:m + STEP, :] = s
            for g in range(STEP // half):
                top = fold(s[g * half:(g + 1) * half], jnp.max)
                best = jnp.maximum(best, jnp.where(order[m // half + g] < pos, top, NEG))
        return best

    def diagonal(t, slot, best):
        own = aligned(ctx, shard)
        lanes = lane_rows(t)
        late = lanes >= half_rows
        offset = jnp.where(late, lanes - half_rows, lanes) // heads
        key = lax.broadcasted_iota(jnp.int32, (shard, 1), 0)
        key_late = key >= half
        key_off = jnp.where(key_late, key - half, key)
        same = key_late == late
        s = sbuf[slot, own, :]
        s = jnp.where(same & (key_off > offset), NEG, s)
        sbuf[slot, own, :] = s
        return jnp.maximum(best, fold(jnp.where(same, s, NEG), jnp.max))

    def weigh(t, slot, best):
        pos = row_pos(t)
        top = jnp.max(best, axis=0, keepdims=True) * EXP_SCALE
        total = jnp.zeros((8, tile), F32)
        mixed = jnp.zeros((8, tile), F32)
        for g in range(n_groups):
            span = pl.ds(g * half, half)
            shift = jnp.where(order[g] <= pos, top, -NEG)
            e = jnp.exp2(sbuf[slot, span, :] * EXP_SCALE - shift)
            sbuf[slot, span, :] = e
            total += fold(e, jnp.sum)
            mixed += fold(e * dpbuf[span, :], jnp.sum)
        scale = 1.0 / jnp.sum(total, axis=0, keepdims=True)
        return scale, jnp.sum(mixed, axis=0, keepdims=True) * scale

    def settle(t, slot, scale, delta):
        out = aligned(t, tile)
        for g in range(n_groups):
            span = pl.ds(g * half, half)
            p = sbuf[slot, span, :] * scale
            ds = p * (dpbuf[span, :] - delta)
            pt[span, out] = p.astype(BF16)
            dst[span, out] = ds.astype(BF16)

    def grad_probs(t):
        for m in range(0, n_keys, STEP):
            dpbuf[m:m + STEP, :] = dot_nt(keys[m:m + STEP, :LAT], do_ref[aligned(t, tile), :])

    best = diagonal(0, 0, scores(0, 0))
    grad_probs(0)

    def one_tile(t, best):
        slot = lax.rem(t, 2)
        scale, delta = weigh(t, slot, best)
        later = scores(t + 1, 1 - slot)
        settle(t, slot, scale, delta)
        grad_probs(t + 1)
        later = diagonal(t + 1, 1 - slot, later)
        return later

    best = lax.fori_loop(0, n_tiles - 1, one_tile, best)
    last = n_tiles - 1
    scale, delta = weigh(last, last % 2, best)
    settle(last, last % 2, scale, delta)

    def dq_out(t):
        return pltpu.make_async_copy(dq_buf.at[lax.rem(t, 2)], dq_hbm.at[aligned(t, tile)], dq_sem.at[t])

    def remote(src, dst, send, recv, device):
        return pltpu.make_async_remote_copy(
            src_ref=src, dst_ref=dst, send_sem=send, recv_sem=recv, device_id=device, device_id_type=MESH)

    def window(q):
        first = jnp.where(q == 0, 0, jnp.where(q == 1, 64, jnp.where(q == 2, 112, 160)))
        return pl.multiple_of(first, 16)

    def to_mate(g):
        return remote(give.at[g], mated.at[g], m_s.at[g], m_r.at[g], mate)

    def x_half(side, g):
        span = pl.ds(side * half, half)
        return remote(sums.at[g, span], x_fwd.at[side], xf_s.at[side], xf_r.at[side], x_peer[1 + 2 * side])

    def x_whole(side, g):
        return remote(sums.at[g], x_full.at[side], xn_s.at[side], xn_r.at[side], x_peer[1 + 2 * side])

    def z_half(side, g):
        span = pl.ds(window(lax.rem(z + 2, 4)) + side * (win // 2), win // 2)
        return remote(sums.at[g, span], z_fwd.at[side, g], zf_s.at[side, g], zf_r.at[side, g], z_peer[1 + 2 * side])

    def z_whole(side, g):
        return remote(z_near.at[side, g], z_full.at[side, g], zn_s.at[side, g], zn_r.at[side, g], z_peer[1 + 2 * side])

    def key_chunk(g, slot):
        for part, kind in ((core, 0), (1 - core, 1)):
            span = aligned(g * 2 + part, shard)
            a = dot(dst[span, :], q_ref[...]) * SCALE
            b = dot(pt[span, :], do_ref[...])
            if kind == 0:
                own_part[slot, :, :LAT] = a[:, :LAT] + b
                own_part[slot, :, LAT:] = a[:, LAT:]
            else:
                give[g, :, :LAT] = (a[:, :LAT] + b).astype(BF16)
                give[g, :, LAT:] = a[:, LAT:].astype(BF16)
        to_mate(g).start()

    def chip_sum(g, slot):
        to_mate(g).wait_recv()
        sums[g] = (own_part[slot] + mated[g].astype(F32)).astype(BF16)

    def z_first(g):
        chip_sum(g, 0)
        z_half(0, g).start()
        z_half(1, g).start()

    def z_second(g):
        for side in range(2):
            base = window(lax.rem(z + 1 + 2 * side, 4))
            near = pl.ds(base + side * (win // 2), win // 2)
            plain = pl.ds(base + (1 - side) * (win // 2), win // 2)
            z_half(side, g).wait_recv()
            mixed = sums[g, near, :].astype(F32) + z_fwd[side, g].astype(F32)
            z_near[side, g, pl.ds(side * (win // 2), win // 2), :] = mixed.astype(BF16)
            z_near[side, g, pl.ds((1 - side) * (win // 2), win // 2), :] = sums[g, plain, :]
            z_whole(side, g).start()

    def column(k):
        return lax.rem(x + jnp.where(k == 0, 2, jnp.where(k == 1, 1, jnp.where(k == 2, 3, 0))), 4)

    def chunk_pair(k, carry):
        col = column(k)
        before = column(lax.rem(k + 3, 4))
        key_chunk(4 + col, 1)

        @pl.when(k > 0)
        def _():
            z_first(before)

        key_chunk(col, 0)
        chip_sum(4 + col, 1)

        @pl.when(k == 0)
        def _():
            x_half(0, 4 + col).start()
            x_half(1, 4 + col).start()

        for side in range(2):
            @pl.when(k == 1 + side)
            def _():
                x_half(side, 4 + col).wait_recv()
                span = pl.ds(side * half, half)
                mixed = sums[4 + col, span, :].astype(F32) + x_fwd[side].astype(F32)
                sums[4 + col, span, :] = mixed.astype(BF16)
                x_whole(side, 4 + col).start()

        @pl.when(k > 0)
        def _():
            z_second(before)

        return carry

    lax.fori_loop(0, 4, chunk_pair, 0)
    z_first(x)

    def second_x(d):
        return remote(a0.at[lax.rem(x + d, 4)], x_two.at[d - 1], x2_s.at[d - 1], x2_r.at[d - 1], x_peer[d])

    def second_z(d):
        span = pl.ds(window(lax.rem(z + d, 4)), win)
        return remote(a1.at[span], z_two.at[d - 1], z2_s.at[d - 1], z2_r.at[d - 1], z_peer[d])

    def across_y(n):
        return remote(halves.at[y_hi if n == 0 else 1 - y_hi], from_y.at[n], y_s.at[n], y_r.at[n], across[n])

    def spread(d):
        return remote(final, from_z.at[d - 1], g_s.at[d - 1], g_r.at[d - 1], z_peer[d])

    def stage_two():
        own_window = pl.ds(window(z), win)

        def gather_z(col, carry):
            total = sums[col, own_window, :].astype(F32)
            for side in range(2):
                z_whole(side, col).wait_recv()
                total += z_full[side, col].astype(F32)
            a0[col] = total.astype(BF16)
            return carry

        lax.fori_loop(0, 4, gather_z, 0)
        total = sums[4 + x].astype(F32)
        for side in range(2):
            x_whole(side, 4 + x).wait_recv()
            total += x_full[side].astype(F32)
        a1[...] = total.astype(BF16)
        for d in (2, 1, 3):
            second_x(d).start()
            second_z(d).start()

    def stage_three():
        low = a0[x].astype(F32)
        high = a1[pl.ds(window(z), win), :].astype(F32)
        for d in (1, 3, 2):
            second_x(d).wait_recv()
            second_z(d).wait_recv()
        for d in (1, 2, 3):
            low += x_two[d - 1].astype(F32)
            high += z_two[d - 1].astype(F32)
        halves[0] = low.astype(BF16)
        halves[1] = high.astype(BF16)
        for n in (2, 1, 0):
            across_y(n).start()

    def stage_four():
        for n in range(3):
            across_y(n).wait_recv()
        near = halves[y_hi].astype(F32) + from_y[0].astype(F32)
        final[...] = (near + (from_y[1].astype(F32) + from_y[2].astype(F32))).astype(BF16)
        for d in (2, 1, 3):
            spread(d).start()

    def query_tile(t, carry):
        @pl.when(t >= 2)
        def _():
            dq_out(t - 2).wait()

        dq_buf[lax.rem(t, 2)] = (dot_tn(dst[:, aligned(t, tile)], keys[...]) * SCALE).astype(BF16)
        dq_out(t).start()
        for when, stage in ((0, lambda: z_second(x)), (2, stage_two), (4, stage_three), (6, stage_four)):
            pl.when(t == when)(stage)
        return carry

    lax.fori_loop(0, n_tiles, query_tile, 0)

    for d in (1, 3, 2):
        spread(d).wait_recv()
    for q, (lo, hi) in enumerate(((0, 64), (64, 112), (112, 160), (160, 224))):
        d = lax.rem(z - q + 4, 4)
        value = final[0:hi - lo].astype(F32)
        for k in range(1, 4):
            value = jnp.where(d == k, from_z[k - 1, 0:hi - lo, :].astype(F32), value)
        dk_ref[lo:hi, :] = value

    for send in sends:
        send.wait_send()
    for copy in passes:
        copy.wait_send()
    for t in (n_tiles - 2, n_tiles - 1):
        dq_out(t).wait()

    def drain(g, carry):
        to_mate(g).wait_send()
        to_mate(4 + g).wait_send()
        for side in range(2):
            z_half(side, g).wait_send()
            z_whole(side, g).wait_send()
        return carry

    lax.fori_loop(0, 4, drain, 0)
    for side in range(2):
        x_half(side, 4 + x).wait_send()
        x_whole(side, 4 + x).wait_send()
    for d in (1, 2, 3):
        second_x(d).wait_send()
        second_z(d).wait_send()
        spread(d).wait_send()
        across_y(d - 1).wait_send()


def per_device(block_order, queries, keys, dout):
    shard, heads, width = queries.shape
    rows = shard * heads
    seq = shard * lax.axis_size("ctx")
    tile, chunk, win = 256, 2 * shard, 64
    any_spec = pl.BlockSpec(memory_space=pl.ANY)
    dma = pltpu.SemaphoreType.DMA

    def half_type(*lead):
        return pltpu.VMEM((*lead, width), BF16)

    grad_queries, key_result = pl.pallas_call(
        functools.partial(attention_kernel, (shard, rows, tile, chunk, win)),
        out_shape=(jax.ShapeDtypeStruct((rows, width), BF16), jax.ShapeDtypeStruct((shard, width), F32)),
        in_specs=[pl.BlockSpec(memory_space=pltpu.SMEM), any_spec, any_spec, any_spec],
        out_specs=[any_spec, pl.BlockSpec(memory_space=pltpu.VMEM)],
        scratch_shapes=[
            half_type(seq), half_type(rows),
            pltpu.VMEM((rows, LAT), BF16),
            pltpu.VMEM((2, seq, tile), F32),
            pltpu.VMEM((seq, tile), F32),
            pltpu.VMEM((seq, rows), BF16),
            pltpu.VMEM((seq, rows), BF16),
            half_type(2, tile),
            pltpu.VMEM((2, shard, width), F32),
            half_type(8, shard), half_type(8, shard), half_type(8, shard),
            half_type(2, shard // 2), half_type(2, shard),
            half_type(2, 4, win // 2), half_type(2, 4, win), half_type(2, 4, win),
            half_type(4, win), half_type(shard), half_type(3, win), half_type(3, win),
            half_type(2, win), half_type(3, win), half_type(win), half_type(3, win),
            dma((3,)), dma((7,)), dma((7,)), dma((8,)), dma((8,)), dma((rows // tile,)),
            dma((8,)), dma((8,)), dma((2,)), dma((2,)), dma((2,)), dma((2,)),
            dma((2, 4)), dma((2, 4)), dma((2, 4)), dma((2, 4)),
            dma((3,)), dma((3,)), dma((3,)), dma((3,)), dma((3,)), dma((3,)), dma((3,)), dma((3,)),
        ],
        compiler_params=pltpu.CompilerParams(collective_id=0, has_side_effects=True, vmem_limit_bytes=62 << 20),
    )(block_order, keys, queries.reshape(rows, width), dout.reshape(rows, LAT))
    return grad_queries.reshape(shard, heads, width), key_result


def solution(mesh):
    placed = (P(), P("ctx", "head", None), P("ctx", None), P("ctx", "head", None))
    return jax.shard_map(
        per_device,
        mesh=mesh,
        in_specs=placed,
        out_specs=(P("ctx", "head", None), P("ctx", None)),
        check_vma=False,
    )
```

time: 154 us -> 123 us (0.80)
  Pallas kernels: 148 us -> 117 us
    pallas_call x1 -> x0, Pallas kernels: 44.8 us -> none  [per_device(): pl.pallas_call(reduce_kernel, out_shape=jax.ShapeDtypeStruct((shard, widt...]
    pallas_call x1, Pallas kernels: 103 us -> 117 us  [per_device(): pl.pallas_call(functools.partial(attention_kernel, (shard, rows, tile, ch...]
    unnamed x6 -> x4, local copies, waits for them, and re-layouts: 4.49 us -> 4.1 us
where the time goes in v2:
time: 123 us; the launch traced here: 122 us
  Pallas kernels  117 us (95%)
  local copies, waits for them, and re-layouts  4.1 us (3%)
    pallas_call x1, Pallas kernels, per_device(): pl.pallas_call(functools.partial(attention_kernel, (shard, rows, tile, ch...  117 us
    unnamed x4, local copies, waits for them, and re-layouts  4.1 us

profile of v2, /device:TPU:0, one launch (start us, length us, event | category | flops | bytes accessed | tf_op | source)
XLA Modules:
  0.0 122.0 jit_solution(7924580480892078990)
XLA Ops:
  0.6 117.2 %shard_map.59 = (bf16[1792,576]{1,0:T(8,128)(2,1)}, f32[224,576]{1,0:T(8,128)}) custom-call(s32[32]{0:T(128)} %order.1, bf16[224,576]{1,0:T(8,128)(2,1)} %own_ref.1, bf16[1792,576]{1,0:T(8,128)(2,1)} %bitcast.3, bf16[1792,512]{1,0:T(8,128)(2,1)} %bitcast.5), custom_call_target="tpu_custom_call" | custom-call | tf_op jit(solution)/shard_map/pallas_call | solution.py:409
  117.9 0.0 copy-start
  117.9 3.3 %copy.8 = bf16[224,8,576]{2,1,0:T(8,128)(2,1)} copy(bf16[224,8,576]{2,1,0:T(8,128)(2,1)} %bitcast.4) | data formatting | bytes 4128768
  121.2 0.0 copy-done
  121.2 0.8 copy.9
Async XLA Ops:
  117.9 3.3 %copy-start = (f32[224,576]{1,0:T(8,128)S(1)}, f32[224,576]{1,0:T(8,128)}, u32[]{:S(2)}) copy-start(f32[224,576]{1,0:T(8,128)} %get-tuple-element.9) | copy-start | bytes 1548292

commit v3 on v2

--- a/solution.py
+++ b/solution.py
@@ -53,7 +53,7 @@
     sizes, order, own_ref, q_hbm, do_hbm, dq_hbm, dk_ref,
     keys, q_ref, do_ref, sbuf, dpbuf, pt, dst, dq_buf,
     own_part, give, mated, sums, x_fwd, x_full, z_fwd, z_near, z_full, a0, a1, z_two, x_two, halves, from_y, final, from_z,
-    in_sem, send_sem, recv_sem, pass_sem, mate_sem, dq_sem,
+    in_sem, send_sem, recv_sem, dq_sem,
     m_s, m_r, xf_s, xf_r, xn_s, xn_r, zf_s, zf_r, zn_s, zn_r, x2_s, x2_r, z2_s, z2_r, y_s, y_r, g_s, g_r,
 ):
     shard, rows, tile, chunk, win = sizes
@@ -72,43 +72,102 @@
     do_in.start()
 
     mate = place(y_hi, x, 1 - core, y_lo, z)
-    steps = [(0, 1), (0, 3), (1, 0), (0, 2), (1, 1), (1, 3), (1, 2)]
-
-    def peer_of(dy, dx):
-        there = (y_hi + dy) % 2, lax.rem(x + dx, 4)
-        return place(*there, core, (y_lo + dy) % 2, z)
-
-    def slot_from(dy, dx):
-        return ((y_hi + dy) % 2) * 8 + lax.rem(x + 4 - dx, 4) * 2 + core
-
     x_peer = [place(y_hi, lax.rem(x + d, 4), core, y_lo, z) for d in range(4)]
     z_peer = [place(y_hi, x, core, y_lo, lax.rem(z + d, 4)) for d in range(4)]
     twin = place(y_hi, x, core, 1 - y_lo, z)
     across = [twin, place(1 - y_hi, x, core, 1 - y_lo, z), place(1 - y_hi, x, core, y_lo, z)]
-    greet([mate, across[0], across[2]] + z_peer[1:] + [peer_of(*step) for step in steps])
+    greet([mate] + across + x_peer[1:] + z_peer[1:])
+
+    win_rows = 32
+    far = shard - 4 * win_rows
+    counter = [0]
+    sent = []
+
+    def move(dy, dx, first, count, device):
+        n = counter[0]
+        counter[0] += 1
+        slot = ((y_hi + dy) % 2) * 8 + lax.rem(x + dx, 4) * 2 + core
+        span = keys.at[pl.ds(pl.multiple_of(slot * shard + first, 16), count)]
+        copy = pltpu.make_async_remote_copy(
+            src_ref=span, dst_ref=span, send_sem=send_sem.at[n], recv_sem=recv_sem.at[n],
+            device_id=device, device_id_type=MESH)
+        copy.start()
+        sent.append(copy)
+        return copy
+
+    def await_all(copies):
+        for copy in copies:
+            copy.wait_recv()
+
+    def window_at(q):
+        return far + q * win_rows
+
+    def near_x(dy):
+        mine = window_at(z)
+        return [[move(dy, 0, mine, win_rows, x_peer[1 + 2 * side]), move(dy, 0, 0, far, x_peer[1 + 2 * side])] for side in range(2)]
+
+    def far_x(dy, side):
+        source = 3 - 2 * side
+        return [
+            move(dy, source, window_at(z) + side * (win_rows // 2), win_rows // 2, x_peer[1 + 2 * side]),
+            move(dy, source, side * (far // 2), far // 2, x_peer[1 + 2 * side])]
+
+    def near_z(dy, dx):
+        return [move(dy, dx, window_at(z), win_rows, z_peer[1 + 2 * side]) for side in range(2)]
+
+    def far_z(dy, dx, arrived):
+        out = []
+        for side in range(2):
+            arrived[side].wait_recv()
+            first = window_at(lax.rem(z + 3 - 2 * side, 4)) + side * (win_rows // 2)
+            out.append(move(dy, dx, first, win_rows // 2, z_peer[1 + 2 * side]))
+        return out
+
     own_in.wait()
-    own_slot = keys.at[aligned(ctx, shard)]
-    sends = []
-    for n, step in enumerate(steps):
-        sends.append(pltpu.make_async_remote_copy(
-            src_ref=own_slot, dst_ref=own_slot, send_sem=send_sem.at[n], recv_sem=recv_sem.at[n],
-            device_id=peer_of(*step), device_id_type=MESH))
-    passes = []
-    for n in range(len(steps) + 1):
-        slot = keys.at[aligned(ctx if n == 0 else slot_from(*steps[n - 1]), shard)]
-        passes.append(pltpu.make_async_remote_copy(
-            src_ref=slot, dst_ref=slot, send_sem=pass_sem.at[n], recv_sem=mate_sem.at[n],
-            device_id=mate, device_id_type=MESH))
-    for send in sends:
-        send.start()
-    passes[0].start()
-    for n in range(len(steps)):
-        sends[n].wait_recv()
-        passes[n + 1].start()
+    over_y = [move(0, 0, window_at(z), win_rows, across[1]), move(0, 0, 0, far, across[1])]
+    over_x = [near_x(0)]
+    mated_keys = [move(0, 0, 0, shard, mate)]
+    around, beyond = {}, {}
+
+    def front(dy, dx):
+        around[dy, dx] = near_z(dy, dx)
+        mated_keys.append(move(dy, dx, 0, far, mate))
+
+    def rest(dy, dx):
+        beyond[dy, dx] = far_z(dy, dx, around[dy, dx])
+
+    await_all(over_y)
+    over_x.append(near_x(1))
+    front(1, 0)
+    far_over_x = []
+    for dy in range(2):
+        halves_x = []
+        for side in range(2):
+            await_all(over_x[dy][side])
+            halves_x += far_x(dy, side)
+            front(dy, 3 - 2 * side)
+        far_over_x.append(halves_x)
+        if dy == 0:
+            rest(1, 0)
+    rest(0, 3)
+    rest(0, 1)
+    await_all(far_over_x[0])
+    front(0, 2)
+    rest(1, 3)
+    rest(1, 1)
+    await_all(far_over_x[1])
+    front(1, 2)
+    for place_of in ((1, 0), (0, 3), (0, 1)):
+        await_all(beyond[place_of])
+        mated_keys.append(move(*place_of, far, 4 * win_rows, mate))
+    rest(0, 2)
+    rest(1, 2)
+    for place_of in ((1, 3), (1, 1), (0, 2), (1, 2)):
+        await_all(beyond[place_of])
+        mated_keys.append(move(*place_of, far, 4 * win_rows, mate))
     q_in.wait()
     do_in.wait()
-    for copy in passes:
-        copy.wait_recv()
+    await_all(mated_keys)
 
     pos_a, pos_b = order[2 * ctx], order[2 * ctx + 1]
     half_rows = rows // 2
@@ -122,18 +181,18 @@
     def fold(value, how):
         return how(value.reshape(value.shape[0] // 8, 8, tile), axis=0)
 
-    def scores(t, slot):
+    step = 896
+
+    def score_step(m, t, buf, best):
         pos = row_pos(t)
-        best = jnp.full((8, tile), NEG, F32)
-        for m in range(0, n_keys, STEP):
-            s = dot_nt(keys[m:m + STEP, :], q_ref[aligned(t, tile), :])
-            sbuf[slot, m:m + STEP, :] = s
-            for g in range(STEP // half):
-                top = fold(s[g * half:(g + 1) * half], jnp.max)
-                best = jnp.maximum(best, jnp.where(order[m // half + g] < pos, top, NEG))
+        s = dot_nt(keys[m:m + step, :], q_ref[aligned(t, tile), :])
+        buf[m:m + step, :] = s
+        for g in range(step // half):
+            top = fold(s[g * half:(g + 1) * half], jnp.max)
+            best = jnp.maximum(best, jnp.where(order[m // half + g] < pos, top, NEG))
         return best
 
-    def diagonal(t, slot, best):
+    def diagonal(t, buf, best):
         own = aligned(ctx, shard)
         lanes = lane_rows(t)
         late = lanes >= half_rows
@@ -142,55 +201,67 @@
         key_late = key >= half
         key_off = jnp.where(key_late, key - half, key)
         same = key_late == late
-        s = sbuf[slot, own, :]
+        s = buf[own, :]
         s = jnp.where(same & (key_off > offset), NEG, s)
-        sbuf[slot, own, :] = s
+        buf[own, :] = s
         return jnp.maximum(best, fold(jnp.where(same, s, NEG), jnp.max))
 
-    def weigh(t, slot, best):
+    def weigh_step(m, t, buf, top, sums_of):
         pos = row_pos(t)
-        top = jnp.max(best, axis=0, keepdims=True) * EXP_SCALE
-        total = jnp.zeros((8, tile), F32)
-        mixed = jnp.zeros((8, tile), F32)
-        for g in range(n_groups):
-            span = pl.ds(g * half, half)
-            shift = jnp.where(order[g] <= pos, top, -NEG)
-            e = jnp.exp2(sbuf[slot, span, :] * EXP_SCALE - shift)
-            sbuf[slot, span, :] = e
+        total, mixed = sums_of
+        for g in range(step // half):
+            span = pl.ds(m + g * half, half)
+            shift = jnp.where(order[m // half + g] <= pos, top, -NEG)
+            e = jnp.exp2(buf[span, :] * EXP_SCALE - shift)
+            buf[span, :] = e
             total += fold(e, jnp.sum)
             mixed += fold(e * dpbuf[span, :], jnp.sum)
-        scale = 1.0 / jnp.sum(total, axis=0, keepdims=True)
-        return scale, jnp.sum(mixed, axis=0, keepdims=True) * scale
-
-    def settle(t, slot, scale, delta):
+        return total, mixed
+
+    def settle_step(m, t, buf, scale, delta):
         out = aligned(t, tile)
-        for g in range(n_groups):
-            span = pl.ds(g * half, half)
-            p = sbuf[slot, span, :] * scale
+        for g in range(step // half):
+            span = pl.ds(m + g * half, half)
+            p = buf[span, :] * scale
             ds = p * (dpbuf[span, :] - delta)
             pt[span, out] = p.astype(BF16)
             dst[span, out] = ds.astype(BF16)
 
-    def grad_probs(t):
-        for m in range(0, n_keys, STEP):
-            dpbuf[m:m + STEP, :] = dot_nt(keys[m:m + STEP, :LAT], do_ref[aligned(t, tile), :])
-
-    best = diagonal(0, 0, scores(0, 0))
-    grad_probs(0)
-
-    def one_tile(t, best):
-        slot = lax.rem(t, 2)
-        scale, delta = weigh(t, slot, best)
-        later = scores(t + 1, 1 - slot)
-        settle(t, slot, scale, delta)
-        grad_probs(t + 1)
-        later = diagonal(t + 1, 1 - slot, later)
-        return later
-
-    best = lax.fori_loop(0, n_tiles - 1, one_tile, best)
-    last = n_tiles - 1
-    scale, delta = weigh(last, last % 2, best)
-    settle(last, last % 2, scale, delta)
+    def probs_step(m, t):
+        dpbuf[m:m + step, :] = dot_nt(keys[m:m + step, :LAT], do_ref[aligned(t, tile), :])
+
+    spans = range(0, n_keys, step)
+    lowest = jnp.full((8, tile), NEG, F32)
+
+    def one_tile(t, now, later, best, more):
+        top = jnp.max(best, axis=0, keepdims=True) * EXP_SCALE
+        parts = jnp.zeros((8, tile), F32), jnp.zeros((8, tile), F32)
+        next_best = lowest
+        for m in spans:
+            parts = weigh_step(m, t, now, top, parts)
+            if more:
+                next_best = score_step(m, t + 1, later, next_best)
+        scale = 1.0 / jnp.sum(parts[0], axis=0, keepdims=True)
+        delta = jnp.sum(parts[1], axis=0, keepdims=True) * scale
+        for m in spans:
+            settle_step(m, t, now, scale, delta)
+            if more:
+                probs_step(m, t + 1)
+        return diagonal(t + 1, later, next_best) if more else None
+
+    best = lowest
+    for m in spans:
+        best = score_step(m, 0, sbuf.at[0], best)
+    best = diagonal(0, sbuf.at[0], best)
+    for m in spans:
+        probs_step(m, 0)
+
+    def two_tiles(n, best):
+        best = one_tile(2 * n, sbuf.at[0], sbuf.at[1], best, True)
+        return one_tile(2 * n + 1, sbuf.at[1], sbuf.at[0], best, True)
+
+    best = lax.fori_loop(0, (n_tiles - 1) // 2, two_tiles, best)
+    one_tile(n_tiles - 1, sbuf.at[0], sbuf.at[1], best, False)
 
     def dq_out(t):
         return pltpu.make_async_copy(dq_buf.at[lax.rem(t, 2)], dq_hbm.at[aligned(t, tile)], dq_sem.at[t])
@@ -203,8 +274,9 @@
         first = jnp.where(q == 0, 0, jnp.where(q == 1, 64, jnp.where(q == 2, 112, 160)))
         return pl.multiple_of(first, 16)
 
-    def to_mate(g):
-        return remote(give.at[g], mated.at[g], m_s.at[g], m_r.at[g], mate)
+    def to_mate(g, k):
+        slot = lax.rem(k, 2) * 2 + g // 4
+        return remote(give.at[slot], mated.at[slot], m_s.at[slot], m_r.at[slot], mate)
 
     def x_half(side, g):
         span = pl.ds(side * half, half)
@@ -220,7 +292,13 @@
     def z_whole(side, g):
         return remote(z_near.at[side, g], z_full.at[side, g], zn_s.at[side, g], zn_r.at[side, g], z_peer[1 + 2 * side])
 
-    def key_chunk(g, slot):
+    def key_chunk(g, slot, k):
+        out = lax.rem(k, 2) * 2 + slot
+
+        @pl.when(k >= 2)
+        def _():
+            to_mate(g, k).wait_send()
+
         for part, kind in ((core, 0), (1 - core, 1)):
             span = aligned(g * 2 + part, shard)
             a = dot(dst[span, :], q_ref[...]) * SCALE
@@ -229,16 +307,16 @@
                 own_part[slot, :, :LAT] = a[:, :LAT] + b
                 own_part[slot, :, LAT:] = a[:, LAT:]
             else:
-                give[g, :, :LAT] = (a[:, :LAT] + b).astype(BF16)
-                give[g, :, LAT:] = a[:, LAT:].astype(BF16)
-        to_mate(g).start()
-
-    def chip_sum(g, slot):
-        to_mate(g).wait_recv()
-        sums[g] = (own_part[slot] + mated[g].astype(F32)).astype(BF16)
-
-    def z_first(g):
-        chip_sum(g, 0)
+                give[out, :, :LAT] = (a[:, :LAT] + b).astype(BF16)
+                give[out, :, LAT:] = a[:, LAT:].astype(BF16)
+        to_mate(g, k).start()
+
+    def chip_sum(g, slot, k):
+        to_mate(g, k).wait_recv()
+        sums[g] = (own_part[slot] + mated[lax.rem(k, 2) * 2 + slot].astype(F32)).astype(BF16)
+
+    def z_first(g, k):
+        chip_sum(g, 0, k)
         z_half(0, g).start()
         z_half(1, g).start()
 
@@ -259,14 +337,14 @@
     def chunk_pair(k, carry):
         col = column(k)
         before = column(lax.rem(k + 3, 4))
-        key_chunk(4 + col, 1)
+        key_chunk(4 + col, 1, k)
 
         @pl.when(k > 0)
         def _():
-            z_first(before)
-
-        key_chunk(col, 0)
-        chip_sum(4 + col, 1)
+            z_first(before, k - 1)
+
+        key_chunk(col, 0, k)
+        chip_sum(4 + col, 1, k)
 
         @pl.when(k == 0)
         def _():
@@ -289,7 +367,7 @@
         return carry
 
     lax.fori_loop(0, 4, chunk_pair, 0)
-    z_first(x)
+    z_first(x, 3)
 
     def second_x(d):
         return remote(a0.at[lax.rem(x + d, 4)], x_two.at[d - 1], x2_s.at[d - 1], x2_r.at[d - 1], x_peer[d])
@@ -369,16 +447,13 @@
             value = jnp.where(d == k, from_z[k - 1, 0:hi - lo, :].astype(F32), value)
         dk_ref[lo:hi, :] = value
 
-    for send in sends:
-        send.wait_send()
-    for copy in passes:
+    for copy in sent:
         copy.wait_send()
     for t in (n_tiles - 2, n_tiles - 1):
         dq_out(t).wait()
 
     def drain(g, carry):
-        to_mate(g).wait_send()
-        to_mate(4 + g).wait_send()
+        to_mate(4 * lax.rem(g, 2), g // 2).wait_send()
         for side in range(2):
             z_half(side, g).wait_send()
             z_whole(side, g).wait_send()
@@ -420,13 +495,13 @@
             pltpu.VMEM((seq, rows), BF16),
             half_type(2, tile),
             pltpu.VMEM((2, shard, width), F32),
-            half_type(8, shard), half_type(8, shard), half_type(8, shard),
+            half_type(4, shard), half_type(4, shard), half_type(8, shard),
             half_type(2, shard // 2), half_type(2, shard),
             half_type(2, 4, win // 2), half_type(2, 4, win), half_type(2, 4, win),
             half_type(4, win), half_type(shard), half_type(3, win), half_type(3, win),
             half_type(2, win), half_type(3, win), half_type(win), half_type(3, win),
-            dma((3,)), dma((7,)), dma((7,)), dma((8,)), dma((8,)), dma((rows // tile,)),
-            dma((8,)), dma((8,)), dma((2,)), dma((2,)), dma((2,)), dma((2,)),
+            dma((3,)), dma((61,)), dma((61,)), dma((rows // tile,)),
+            dma((4,)), dma((4,)), dma((2,)), dma((2,)), dma((2,)), dma((2,)),
             dma((2, 4)), dma((2, 4)), dma((2, 4)), dma((2, 4)),
             dma((3,)), dma((3,)), dma((3,)), dma((3,)), dma((3,)), dma((3,)), dma((3,)), dma((3,)),
         ],

time: 123 us -> 112 us (0.911)
  Pallas kernels: 117 us -> 106 us
    pallas_call x1, Pallas kernels: 117 us -> 106 us  [per_device(): pl.pallas_call(functools.partial(attention_kernel, (shard, rows, tile, ch...]
where the time goes in v3:
time: 112 us; the launch traced here: 111 us
  Pallas kernels  106 us (95%)
  local copies, waits for them, and re-layouts  4.1 us (4%)
    pallas_call x1, Pallas kernels, per_device(): pl.pallas_call(functools.partial(attention_kernel, (shard, rows, tile, ch...  106 us
    unnamed x4, local copies, waits for them, and re-layouts  4.1 us

profile of v3, /device:TPU:0, one launch (start us, length us, event | category | flops | bytes accessed | tf_op | source)
XLA Modules:
  0.0 110.9 jit_solution(15420020972972919179)
XLA Ops:
  0.6 106.2 %shard_map.59 = (bf16[1792,576]{1,0:T(8,128)(2,1)}, f32[224,576]{1,0:T(8,128)}) custom-call(s32[32]{0:T(128)} %order.1, bf16[224,576]{1,0:T(8,128)(2,1)} %own_ref.1, bf16[1792,576]{1,0:T(8,128)(2,1)} %bitcast.3, bf16[1792,512]{1,0:T(8,128)(2,1)} %bitcast.5), custom_call_target="tpu_custom_call" | custom-call | tf_op jit(solution)/shard_map/pallas_call | solution.py:484
  106.8 0.0 copy-start
  106.8 3.3 %copy.8 = bf16[224,8,576]{2,1,0:T(8,128)(2,1)} copy(bf16[224,8,576]{2,1,0:T(8,128)(2,1)} %bitcast.4) | data formatting | bytes 4128768
  110.1 0.0 copy-done
  110.1 0.8 copy.9
Async XLA Ops:
  106.8 3.3 %copy-start = (f32[224,576]{1,0:T(8,128)S(1)}, f32[224,576]{1,0:T(8,128)}, u32[]{:S(2)}) copy-start(f32[224,576]{1,0:T(8,128)} %get-tuple-element.9) | copy-start | bytes 1548292

commit v4 on v3

--- a/solution.py
+++ b/solution.py
@@ -102,15 +102,19 @@
     def window_at(q):
         return far + q * win_rows
 
-    def near_x(dy):
-        mine = window_at(z)
-        return [[move(dy, 0, mine, win_rows, x_peer[1 + 2 * side]), move(dy, 0, 0, far, x_peer[1 + 2 * side])] for side in range(2)]
-
-    def far_x(dy, side):
-        source = 3 - 2 * side
-        return [
-            move(dy, source, window_at(z) + side * (win_rows // 2), win_rows // 2, x_peer[1 + 2 * side]),
-            move(dy, source, side * (far // 2), far // 2, x_peer[1 + 2 * side])]
+    def step_of(rows_of):
+        return (window_at(z), win_rows) if rows_of == "window" else (0, far)
+
+    def near_x(dy, rows_of):
+        return [move(dy, 0, *step_of(rows_of), x_peer[1 + 2 * side]) for side in range(2)]
+
+    def far_x(dy, rows_of, arrived):
+        out = []
+        for side in range(2):
+            arrived[side].wait_recv()
+            first, count = step_of(rows_of)
+            out.append(move(dy, 3 - 2 * side, first + side * (count // 2), count // 2, x_peer[1 + 2 * side]))
+        return out
 
     def near_z(dy, dx):
         return [move(dy, dx, window_at(z), win_rows, z_peer[1 + 2 * side]) for side in range(2)]
@@ -123,48 +127,58 @@
             out.append(move(dy, dx, first, win_rows // 2, z_peer[1 + 2 * side]))
         return out
 
+    around, beyond, mated_keys = {}, {}, []
+
+    def round_z(*sources):
+        for source in sources:
+            around[source] = near_z(*source)
+
+    def round_z_again(*sources):
+        for source in sources:
+            beyond[source] = far_z(*source, around[source])
+
+    def hand_over(first, count, *sources):
+        for source in sources:
+            mated_keys.append(move(*source, first, count, mate))
+
+    def hand_over_windows(*sources):
+        for source in sources:
+            await_all(beyond[source])
+            hand_over(far, 4 * win_rows, source)
+
     own_in.wait()
-    over_y = [move(0, 0, window_at(z), win_rows, across[1]), move(0, 0, 0, far, across[1])]
-    over_x = [near_x(0)]
-    mated_keys = [move(0, 0, 0, shard, mate)]
-    around, beyond = {}, {}
-
-    def front(dy, dx):
-        around[dy, dx] = near_z(dy, dx)
-        mated_keys.append(move(dy, dx, 0, far, mate))
-
-    def rest(dy, dx):
-        beyond[dy, dx] = far_z(dy, dx, around[dy, dx])
-
-    await_all(over_y)
-    over_x.append(near_x(1))
-    front(1, 0)
-    far_over_x = []
-    for dy in range(2):
-        halves_x = []
-        for side in range(2):
-            await_all(over_x[dy][side])
-            halves_x += far_x(dy, side)
-            front(dy, 3 - 2 * side)
-        far_over_x.append(halves_x)
-        if dy == 0:
-            rest(1, 0)
-    rest(0, 3)
-    rest(0, 1)
-    await_all(far_over_x[0])
-    front(0, 2)
-    rest(1, 3)
-    rest(1, 1)
-    await_all(far_over_x[1])
-    front(1, 2)
-    for place_of in ((1, 0), (0, 3), (0, 1)):
-        await_all(beyond[place_of])
-        mated_keys.append(move(*place_of, far, 4 * win_rows, mate))
-    rest(0, 2)
-    rest(1, 2)
-    for place_of in ((1, 3), (1, 1), (0, 2), (1, 2)):
-        await_all(beyond[place_of])
-        mated_keys.append(move(*place_of, far, 4 * win_rows, mate))
+    y_window = move(0, 0, window_at(z), win_rows, across[1])
+    x_window = [near_x(0, "window")]
+    y_window.wait_recv()
+    x_window.append(near_x(1, "window"))
+    round_z((1, 0))
+    x_window_far = [far_x(0, "window", x_window[0])]
+    round_z((0, 3), (0, 1))
+    y_rest = move(0, 0, 0, far, across[1])
+    x_rest = [near_x(0, "rest")]
+    hand_over(0, shard, (0, 0))
+    x_window_far.append(far_x(1, "window", x_window[1]))
+    round_z((1, 3), (1, 1))
+    await_all(x_window_far[0])
+    round_z((0, 2))
+    round_z_again((1, 0))
+    await_all(x_window_far[1])
+    round_z((1, 2))
+    round_z_again((0, 3), (0, 1))
+    y_rest.wait_recv()
+    x_rest.append(near_x(1, "rest"))
+    hand_over(0, far, (1, 0))
+    x_rest_far = [far_x(0, "rest", x_rest[0])]
+    hand_over(0, far, (0, 3), (0, 1))
+    round_z_again((1, 3), (1, 1), (0, 2), (1, 2))
+    hand_over_windows((1, 0), (0, 3), (0, 1))
+    x_rest_far.append(far_x(1, "rest", x_rest[1]))
+    hand_over(0, far, (1, 3), (1, 1))
+    await_all(x_rest_far[0])
+    hand_over(0, far, (0, 2))
+    hand_over_windows((1, 3), (1, 1), (0, 2), (1, 2))
+    await_all(x_rest_far[1])
+    hand_over(0, far, (1, 2))
     q_in.wait()
     do_in.wait()
     await_all(mated_keys)
@@ -299,16 +313,13 @@
         def _():
             to_mate(g, k).wait_send()
 
-        for part, kind in ((core, 0), (1 - core, 1)):
-            span = aligned(g * 2 + part, shard)
-            a = dot(dst[span, :], q_ref[...]) * SCALE
-            b = dot(pt[span, :], do_ref[...])
-            if kind == 0:
-                own_part[slot, :, :LAT] = a[:, :LAT] + b
-                own_part[slot, :, LAT:] = a[:, LAT:]
-            else:
-                give[out, :, :LAT] = (a[:, :LAT] + b).astype(BF16)
-                give[out, :, LAT:] = a[:, LAT:].astype(BF16)
+        kept, given = aligned(g * 2 + core, shard), aligned(g * 2 + 1 - core, shard)
+        a = dot(jnp.concatenate([dst[kept, :], dst[given, :]]), q_ref[...]) * SCALE
+        b = dot(jnp.concatenate([pt[kept, :], pt[given, :]]), do_ref[...])
+        own_part[slot, :, :LAT] = a[:shard, :LAT] + b[:shard]
+        own_part[slot, :, LAT:] = a[:shard, LAT:]
+        give[out, :, :LAT] = (a[shard:, :LAT] + b[shard:]).astype(BF16)
+        give[out, :, LAT:] = a[shard:, LAT:].astype(BF16)
         to_mate(g, k).start()
 
     def chip_sum(g, slot, k):
@@ -337,14 +348,18 @@
     def chunk_pair(k, carry):
         col = column(k)
         before = column(lax.rem(k + 3, 4))
-        key_chunk(4 + col, 1, k)
+        @pl.when(k < 3)
+        def _():
+            key_chunk(4 + col, 1, k)
 
         @pl.when(k > 0)
         def _():
             z_first(before, k - 1)
 
         key_chunk(col, 0, k)
-        chip_sum(4 + col, 1, k)
+        @pl.when(k < 3)
+        def _():
+            chip_sum(4 + col, 1, k)
 
         @pl.when(k == 0)
         def _():
@@ -367,6 +382,7 @@
         return carry
 
     lax.fori_loop(0, 4, chunk_pair, 0)
+    key_chunk(4 + x, 1, 3)
     z_first(x, 3)
 
     def second_x(d):
@@ -425,6 +441,10 @@
         for d in (2, 1, 3):
             spread(d).start()
 
+    def last_sums():
+        z_second(x)
+        chip_sum(4 + x, 1, 3)
+
     def query_tile(t, carry):
         @pl.when(t >= 2)
         def _():
@@ -432,7 +452,7 @@
 
         dq_buf[lax.rem(t, 2)] = (dot_tn(dst[:, aligned(t, tile)], keys[...]) * SCALE).astype(BF16)
         dq_out(t).start()
-        for when, stage in ((0, lambda: z_second(x)), (2, stage_two), (4, stage_three), (6, stage_four)):
+        for when, stage in ((0, last_sums), (2, stage_two), (4, stage_three), (6, stage_four)):
             pl.when(t == when)(stage)
         return carry
 
@@ -505,7 +525,7 @@
             dma((2, 4)), dma((2, 4)), dma((2, 4)), dma((2, 4)),
             dma((3,)), dma((3,)), dma((3,)), dma((3,)), dma((3,)), dma((3,)), dma((3,)), dma((3,)),
         ],
-        compiler_params=pltpu.CompilerParams(collective_id=0, has_side_effects=True, vmem_limit_bytes=62 << 20),
+        compiler_params=pltpu.CompilerParams(collective_id=0, has_side_effects=True, vmem_limit_bytes=63 << 20),
     )(block_order, keys, queries.reshape(rows, width), dout.reshape(rows, LAT))
     return grad_queries.reshape(shard, heads, width), key_result
 

time: 112 us -> 108 us (0.964)
  Pallas kernels: 106 us -> 103 us
    pallas_call x1, Pallas kernels: 106 us -> 103 us  [per_device(): pl.pallas_call(functools.partial(attention_kernel, (shard, rows, tile, ch...]
where the time goes in v4:
time: 108 us
  Pallas kernels  103 us (95%)
  local copies, waits for them, and re-layouts  4.1 us (4%)
    pallas_call x1, Pallas kernels, per_device(): pl.pallas_call(functools.partial(attention_kernel, (shard, rows, tile, ch...  103 us
    unnamed x4, local copies, waits for them, and re-layouts  4.1 us

profile of v4, /device:TPU:0, one launch (start us, length us, event | category | flops | bytes accessed | tf_op | source)
XLA Modules:
  0.0 107.9 jit_solution(9367567426484919507)
XLA Ops:
  0.6 103.2 %shard_map.59 = (bf16[1792,576]{1,0:T(8,128)(2,1)}, f32[224,576]{1,0:T(8,128)}) custom-call(s32[32]{0:T(128)} %order.1, bf16[224,576]{1,0:T(8,128)(2,1)} %own_ref.1, bf16[1792,576]{1,0:T(8,128)(2,1)} %bitcast.3, bf16[1792,512]{1,0:T(8,128)(2,1)} %bitcast.5), custom_call_target="tpu_custom_call" | custom-call | tf_op jit(solution)/shard_map/pallas_call | solution.py:504
  103.8 0.0 copy-start
  103.8 3.3 %copy.8 = bf16[224,8,576]{2,1,0:T(8,128)(2,1)} copy(bf16[224,8,576]{2,1,0:T(8,128)(2,1)} %bitcast.4) | data formatting | bytes 4128768
  107.1 0.0 copy-done
  107.1 0.8 copy.9
Async XLA Ops:
  103.8 3.3 %copy-start = (f32[224,576]{1,0:T(8,128)S(1)}, f32[224,576]{1,0:T(8,128)}, u32[]{:S(2)}) copy-start(f32[224,576]{1,0:T(8,128)} %get-tuple-element.9) | copy-start | bytes 1548292

commit v5 on v4

--- a/solution.py
+++ b/solution.py
@@ -12,6 +12,7 @@
 EXP_SCALE = SCALE * LOG2E
 NEG = -1e30
 LAT = 512
+PIECES = 2
 STEP = 896
 MESH = pl.DeviceIdType.MESH
 BF16, F32 = jnp.bfloat16, jnp.float32
@@ -490,6 +491,11 @@
         across_y(d - 1).wait_send()
 
 
+def hand_on_kernel(dq_ref, dk_ref, dq_out, dk_out):
+    dq_out[...] = dq_ref[...]
+    dk_out[...] = dk_ref[...]
+
+
 def per_device(block_order, queries, keys, dout):
     shard, heads, width = queries.shape
     rows = shard * heads
@@ -527,6 +533,14 @@
         ],
         compiler_params=pltpu.CompilerParams(collective_id=0, has_side_effects=True, vmem_limit_bytes=63 << 20),
     )(block_order, keys, queries.reshape(rows, width), dout.reshape(rows, LAT))
+    blocks = [pl.BlockSpec((rows // PIECES, width), lambda n: (n, 0)), pl.BlockSpec((shard // PIECES, width), lambda n: (n, 0))]
+    grad_queries, key_result = pl.pallas_call(
+        hand_on_kernel,
+        grid=(PIECES,),
+        out_shape=(jax.ShapeDtypeStruct((rows, width), BF16), jax.ShapeDtypeStruct((shard, width), F32)),
+        in_specs=blocks,
+        out_specs=blocks,
+    )(grad_queries, key_result)
     return grad_queries.reshape(shard, heads, width), key_result
 
 

time: 108 us -> 107 us (level)
  local copies, waits for them, and re-layouts: 4.1 us -> 0 us
  Pallas kernels: 103 us -> 106 us
    unnamed x4 -> x0, local copies, waits for them, and re-layouts: 4.1 us -> none
    pallas_call x0 -> x1, Pallas kernels: none -> 2.98 us  [per_device(): pl.pallas_call(hand_on_kernel, grid=(PIECES,), out_shape=(jax.ShapeDtypeS...]
where the time goes in v5:
time: 107 us
  Pallas kernels  106 us (99%)
    pallas_call x1, Pallas kernels, per_device(): pl.pallas_call(functools.partial(attention_kernel, (shard, rows, tile, ch...  103 us
    pallas_call x1, Pallas kernels, per_device(): pl.pallas_call(hand_on_kernel, grid=(PIECES,), out_shape=(jax.ShapeDtypeS...  2.98 us

profile of v5, /device:TPU:0, one launch (start us, length us, event | category | flops | bytes accessed | tf_op | source)
XLA Modules:
  0.0 106.8 jit_solution(16451807691267845602)
XLA Ops:
  0.6 103.2 %shard_map.59 = (bf16[1792,576]{1,0:T(8,128)(2,1)}, f32[224,576]{1,0:T(8,128)}) custom-call(s32[32]{0:T(128)} %order.1, bf16[224,576]{1,0:T(8,128)(2,1)} %own_ref.1, bf16[1792,576]{1,0:T(8,128)(2,1)} %bitcast.3, bf16[1792,512]{1,0:T(8,128)(2,1)} %bitcast.4), custom_call_target="tpu_custom_call" | custom-call | tf_op jit(solution)/shard_map/pallas_call | solution.py:510
  103.8 3.0 %shard_map.60 = (bf16[1792,576]{1,0:T(8,128)(2,1)}, f32[224,576]{1,0:T(8,128)}) custom-call(bf16[1792,576]{1,0:T(8,128)(2,1)} %get-tuple-element.6.dq_ref, f32[224,576]{1,0:T(8,128)} %get-tuple-element.7.dk_ref), custom_call_target="tpu_custom_call" | custom-call | tf_op jit(solution)/shard_map/pallas_call | solution.py:537
